TPU v7x, 32 devices: a whole 2x2x4 slice. The times are simulated.
32 devices in a mesh: vol: 1, slab: 8 (over z, x), filt: 4 (over y, core).
Axes of the slice: x: 2, y: 2, z: 4, core: 2. Of those that a mesh axis runs over, the one named last changes fastest.
Arguments:
- volume: bfloat16 [32, 64, 64, 256], P(('vol', 'slab', 'filt')), may hold values from -6 to 6
- weights: bfloat16 [256, 27, 256], P('filt'), may hold values from -0.078125 to 0.078125
- bias: bfloat16 [256], P('filt'), may hold values from -3 to 3
Outputs:
- activated: bfloat16 [32, 64, 64, 256], P(('vol', 'slab'), None, None, 'filt')
All inputs are finite; a program needn't handle non-finite values.
Results may differ from a plain program's by a relative error of at most 0.001.
Values may be sent and summed in bfloat16 or wider, within the bound.
A program may use at most 448 MiB of HBM per device.

v0:
```python
import jax
import jax.numpy as jnp
from jax import lax
from jax.sharding import PartitionSpec as P


def extended(cells, sides, width):
    for axis, dim in sides:
        count = lax.axis_size(axis)
        ends = count - 1
        head = lax.slice_in_dim(cells, 0, width, axis=dim)
        tail = lax.slice_in_dim(cells, cells.shape[dim] - width, cells.shape[dim], axis=dim)
        cells = jnp.concatenate(
            [
                lax.ppermute(tail, axis, [(i, (i + 1) % count) for i in range(ends)]),
                cells,
                lax.ppermute(head, axis, [((i + 1) % count, i) for i in range(ends)]),
            ],
            axis=dim,
        )
    return cells


def convolve(padded, weights, bias):
    planes = padded.shape[0] - 2
    rows = padded.shape[1]
    cols = padded.shape[2]
    chans = padded.shape[3]
    outs = weights.shape[0]
    framed = jnp.pad(padded, ((0, 0), (1, 1), (1, 1), (0, 0)))
    total = jnp.zeros((planes, rows * cols, outs), jnp.float32)
    for tap_z in range(3):
        for tap_y in range(3):
            for tap_x in range(3):
                window = framed[
                    tap_z : tap_z + planes, tap_y : tap_y + rows, tap_x : tap_x + cols
                ].reshape(planes, rows * cols, chans)
                tap_weight = weights[:, 9 * tap_z + 3 * tap_y + tap_x, :]
                total = total + jnp.einsum(
                    "zpi,oi->zpo", window, tap_weight, preferred_element_type=jnp.float32
                )
    shifted = total + bias.astype(jnp.float32)[None, None, :]
    result = jnp.where(shifted > 0, shifted, 0.3 * shifted)
    return result.astype(jnp.bfloat16).reshape(planes, rows, cols, outs)


def body(volume, weights, bias):
    slab_planes = lax.all_gather(volume, "filt", axis=0, tiled=True)
    padded = extended(slab_planes, (("slab", 0),), 1)
    return convolve(padded, weights, bias)


def solution(mesh):
    return jax.shard_map(
        body,
        mesh=mesh,
        in_specs=(P(("vol", "slab", "filt"), None, None, None), P("filt", None, None), P("filt")),
        out_specs=P(("vol", "slab"), None, None, "filt"),
        check_vma=False,
    )
```

profile of v0, /device:TPU:4, one launch (start us, length us, event | category | flops | bytes accessed | tf_op | source)
XLA Modules:
  0.0 521.9 jit_solution(2084521685995472989)
XLA Ops:
  7.3 60.0 %all-gather.2.cloned.1.call-done = bf16[4,64,64,256]{3,2,1,0:T(8,128)(2,1)} async-done(((bf16[1,64,64,256]{3,2,1,0:T(8,128)(2,1)}), bf16[4,64,64,256]{3,2,1,0:T(8,128)(2,1)}) %all-gather.2.cloned.1.call-update) | async-done | bytes 8388624 | tf_op jit(solution)/shard_map/all_gather | solution.py:48
  75.9 4.6 fusion.57
  80.5 83.6 %collective-permute-done = bf16[1,64,64,256]{3,2,1,0:T(8,128)(2,1)S(1)} collective-permute-done((bf16[1,64,64,256]{3,2,1,0:T(8,128)(2,1)S(1)}, bf16[1,64,64,256]{3,2,1,0:T(8,128)(2,1)S(1)}, u32[]{:S(2)}, u32[]{:S(2)}) %collective-permute-start) | collective-permute-done | bytes 2097184 | tf_op jit(solution)/shard_map/ppermute | solution.py:15
  166.9 21.5 %select_maximum_fusion = bf16[6,66,66,256]{3,2,1,0:T(8,128)(2,1)} fusion(bf16[1,64,64,256]{3,2,1,0:T(8,128)(2,1)S(1)} %collective-permute-done.1, bf16[4,64,64,256]{3,2,1,0:T(8,128)(2,1)S(1)} %copy-done, bf16[1,64,64,256]{3,2,1,0:T(8,128)(2,1)S(1)} %collective-permute-done), kind=kLoop, calls=%fused_computation.7 | loop fusion | flops 127125504 | bytes 25964544 | tf_op jit(solution)/shard_map/concatenate | solution.py:13
  188.4 126.1 %fusion.111 = (bf16[4,64,64,256]{3,2,1,0:T(8,128)(2,1)}, bf16[4,64,64,256]{3,2,1,0:T(8,128)(2,1)}, bf16[4,64,64,256]{3,2,1,0:T(8,128)(2,1)}, bf16[4,64,64,256]{3...) fusion(bf16[6,66,66,256]{3,2,1,0:T(8,128)(2,1)} %select_maximum, ...), kind=kLoop, calls=%fused_computation.122 | loop fusion | bytes 318767104 | tf_op jit(solution)/shard_map/slice | solution.py:35
  314.5 32.3 %fusion.112 = (bf16[4,64,64,256]{3,2,1,0:T(8,128)(2,1)}, bf16[4,64,64,256]{3,2,1,0:T(8,128)(2,1)}, bf16[4,64,64,256]{3,2,1,0:T(8,128)(2,1)}, bf16[4,64,64,256]{3,2,1,0:T(8,128)(2,1)}, bf16[4,64,64,256]{3,2,1,0:T(8,128)(2,1)}) fusion(bf16[6,66,66,256]{3,2,1,0:T(8,128)(2,1)} %select_maximum_fusion), kind=kLoop, calls=%fused_computation.123 | loop fusion | bytes 83886080 | tf_op jit(solution)/shard_map/slice | solution.py:35
  346.8 8.2 %fusion.59 = f32[4,4096,64]{1,2,0:T(8,128)} fusion(bf16[4,4096,256]{2,1,0:T(8,128)(2,1)} %bitcast.221, bf16[64,27,256]{2,0,1:T(8,128)(2,1)S(1)} %copy-done.6), kind=kOutput, calls=%fused_computation.70 | convolution fusion | flops 536870912 | bytes 12615680 | tf_op jit(solution)/shard_map/zpi,oi->zpo/dot_general | solution.py:39
  355.0 4.6 fusion.61
  359.7 4.7 fusion.63
  364.4 4.6 fusion.65
  369.1 4.7 fusion.67
  373.7 4.6 fusion.69
  378.3 4.7 fusion.71
  383.0 4.6 fusion.73
  387.6 4.7 fusion.77
  392.4 4.6 fusion.79
  397.0 4.8 fusion.81
  406.2 4.6 fusion.75
  410.8 4.6 fusion.34
  415.4 4.6 fusion.36
  420.0 4.6 fusion.38
  424.6 4.6 fusion.42
  429.2 4.6 fusion.44
  433.8 4.6 fusion.46
  443.0 4.7 fusion.50
  447.7 4.6 fusion.52
  452.4 4.6 fusion.54
  456.9 4.7 fusion.32
  461.6 4.6 fusion.40
  466.2 24.2 %fusion.29 = f32[4,4096,64]{1,2,0:T(8,128)} fusion(f32[4,4096,64]{1,2,0:T(8,128)} %fusion.57, f32[4,4096,64]{1,2,0:T(8,128)} %fusion.59, f32[4,4096,64]{1,2,0:T(8,128)} %fusion.61, f32[4,4096,64]{1,2,0:T(8,128)} %fusion.63, f32[4,4096,64]{1,2,0:T(8,128)} %fusion.65, f32[4,4096,64]{1,2,0:T(8,128)} %fusion.67, f32[4,4096,64]{1,2,0:T(8,128)} %fusion.69, ...), kind=kOutput, calls=%fused_computation.40 | convolution fusion | flops 550502400 | bytes 67141632 | tf_op jit(solution)/shard_map/zpi,oi->zpo/dot_general | solution.py:39
  490.4 19.7 %fusion.31 = bf16[4,4096,64]{1,2,0:T(8,128)(2,1)} fusion(f32[4,4096,64]{1,2,0:T(8,128)} %fusion.32, f32[4,4096,64]{1,2,0:T(8,128)} %fusion.34, f32[4,4096,64]{1,2,0:T(8,128)} %fusion.36, f32[4,4096,64]{1,2,0:T(8,128)} %fusion.38, f32[4,4096,64]{1,2,0:T(8,128)} %fusion.40, f32[4,4096,64]{1,2,0:T(8,128)} %fusion.42, f32[4,4096,64]{1,2,0:T(8,128)} %fusion.44, ...), kind=kOutput, calls=%fused_computation.42 | convolution fusion | flops 555745280 | bytes 65044992 | tf_op jit(solution)/shard_map/zpi,oi->zpo/dot_general | solution.py:39
  510.1 4.8 copy.6
  (142 shorter events, 21.3 us)
Async XLA Ops:
  6.5 68.8 %copy-start.8 = (bf16[64]{0:T(256)(128)(2,1)S(1)}, bf16[64]{0:T(256)(128)(2,1)}, u32[]{:S(2)}) copy-start(bf16[64]{0:T(256)(128)(2,1)} %param.5) | copy-start | bytes 388
  6.5 69.4 %copy-start.6 = (bf16[64,27,256]{2,0,1:T(8,128)(2,1)S(1)}, bf16[64,27,256]{2,0,1:T(8,128)(2,1)}, u32[]{:S(2)}) copy-start(bf16[64,27,256]{2,0,1:T(8,128)(2,1)} %param.4) | copy-start | bytes 2654212
  6.5 60.8 %all-gather.2.cloned.1.call-start = ((), (), s32[]{:S(2)}) async-start(), calls=%async_computation | async-start | bytes 10485760 | tf_op jit(solution)/shard_map/all_gather | solution.py:48
  67.3 8.7 %copy-start = (bf16[4,64,64,256]{3,2,1,0:T(8,128)(2,1)S(1)}, bf16[4,64,64,256]{3,2,1,0:T(8,128)(2,1)}, u32[]{:S(2)}) copy-start(bf16[4,64,64,256]{3,2,1,0:T(8,128)(2,1)} %all-gather.2.cloned.1.call-done) | copy-start | bytes 25165828
  70.2 94.0 %collective-permute-start = (bf16[1,64,64,256]{3,2,1,0:T(8,128)(2,1)S(1)}, bf16[1,64,64,256]{3,2,1,0:T(8,128)(2,1)S(1)}, u32[]{:S(2)}, u32[]{:S(2)}) collective-permute-start(bf16[1,64,64,256]{3,2,1,0:T(8,128)(2,1)S(1)} %get-tuple-element.31), channel_id=1, source_target_pairs={{0,4},{4,8},{8,12},{12,16},{16,20},{20,24},{24,28},{1,5},{5,9},{9,... | collective-permute-start | bytes 6291464 | tf_op jit(solution)/shard_map/ppermute | solution.py:15
  74.1 90.1 %collective-permute-start.1 = (bf16[1,64,64,256]{3,2,1,0:T(8,128)(2,1)S(1)}, bf16[1,64,64,256]{3,2,1,0:T(8,128)(2,1)S(1)}, u32[]{:S(2)}, u32[]{:S(2)}) collective-permute-start(bf16[1,64,64,256]{3,2,1,0:T(8,128)(2,1)S(1)} %get-tuple-element.32), channel_id=1, source_target_pairs={{4,0},{8,4},{12,8},{16,12},{20,16},{24,20},{28,24},{5,1},{9,5},{13... | collective-permute-start | bytes 6291464 | tf_op jit(solution)/shard_map/ppermute | solution.py:17
  346.8 12.8 %slice-start.34 = ((s8[8388608]{0:T(1024)(128)(4,1)}), s8[4194304]{0:T(1024)(128)(4,1)S(1)}, s32[]{:S(2)}) async-start(s8[8388608]{0:T(1024)(128)(4,1)} %bitcast.214), calls=%async_computation.35 | async-start | bytes 8388608
  355.0 9.4 %slice-start.32 = ((s8[8388608]{0:T(1024)(128)(4,1)}), s8[4194304]{0:T(1024)(128)(4,1)S(1)}, s32[]{:S(2)}) async-start(s8[8388608]{0:T(1024)(128)(4,1)} %bitcast.211), calls=%async_computation.33 | async-start | bytes 8388608
  359.7 9.4 %slice-start.30 = ((s8[8388608]{0:T(1024)(128)(4,1)}), s8[4194304]{0:T(1024)(128)(4,1)S(1)}, s32[]{:S(2)}) async-start(s8[8388608]{0:T(1024)(128)(4,1)} %bitcast.208), calls=%async_computation.31 | async-start | bytes 8388608
  364.4 9.3 %slice-start.28 = ((s8[8388608]{0:T(1024)(128)(4,1)}), s8[4194304]{0:T(1024)(128)(4,1)S(1)}, s32[]{:S(2)}) async-start(s8[8388608]{0:T(1024)(128)(4,1)} %bitcast.205), calls=%async_computation.29 | async-start | bytes 8388608
  369.0 9.3 %slice-start.26 = ((s8[8388608]{0:T(1024)(128)(4,1)}), s8[4194304]{0:T(1024)(128)(4,1)S(1)}, s32[]{:S(2)}) async-start(s8[8388608]{0:T(1024)(128)(4,1)} %bitcast.202), calls=%async_computation.27 | async-start | bytes 8388608
  373.7 9.3 %slice-start.24 = ((s8[8388608]{0:T(1024)(128)(4,1)}), s8[4194304]{0:T(1024)(128)(4,1)S(1)}, s32[]{:S(2)}) async-start(s8[8388608]{0:T(1024)(128)(4,1)} %bitcast.199), calls=%async_computation.25 | async-start | bytes 8388608
  378.3 9.3 %slice-start.42 = ((s8[8388608]{0:T(1024)(128)(4,1)}), s8[4194304]{0:T(1024)(128)(4,1)S(1)}, s32[]{:S(2)}) async-start(s8[8388608]{0:T(1024)(128)(4,1)} %bitcast.228), calls=%async_computation.43 | async-start | bytes 8388608
  383.0 9.4 %slice-start.40 = ((s8[8388608]{0:T(1024)(128)(4,1)}), s8[4194304]{0:T(1024)(128)(4,1)S(1)}, s32[]{:S(2)}) async-start(s8[8388608]{0:T(1024)(128)(4,1)} %bitcast.225), calls=%async_computation.41 | async-start | bytes 8388608
  387.6 9.4 %slice-start.38 = ((s8[8388608]{0:T(1024)(128)(4,1)}), s8[4194304]{0:T(1024)(128)(4,1)S(1)}, s32[]{:S(2)}) async-start(s8[8388608]{0:T(1024)(128)(4,1)} %bitcast.222), calls=%async_computation.39 | async-start | bytes 8388608
  392.4 9.4 %slice-start = ((s8[8388608]{0:T(1024)(128)(4,1)}), s8[4194304]{0:T(1024)(128)(4,1)S(1)}, s32[]{:S(2)}) async-start(s8[8388608]{0:T(1024)(128)(4,1)} %bitcast.164), calls=%async_computation.1 | async-start | bytes 8388608
  397.0 13.8 %slice-start.22 = ((s8[8388608]{0:T(1024)(128)(4,1)}), s8[4194304]{0:T(1024)(128)(4,1)S(1)}, s32[]{:S(2)}) async-start(s8[8388608]{0:T(1024)(128)(4,1)} %bitcast.196), calls=%async_computation.23 | async-start | bytes 8388608
  401.8 9.0 %slice-start.23 = ((s8[8388608]{0:T(1024)(128)(4,1)}), s8[4194304]{0:T(1024)(128)(4,1)S(1)}, s32[]{:S(2)}) async-start(s8[8388608]{0:T(1024)(128)(4,1)} %bitcast.196), calls=%async_computation.24 | async-start | bytes 8388608
  406.2 9.2 %slice-start.20 = ((s8[8388608]{0:T(1024)(128)(4,1)}), s8[4194304]{0:T(1024)(128)(4,1)S(1)}, s32[]{:S(2)}) async-start(s8[8388608]{0:T(1024)(128)(4,1)} %bitcast.193), calls=%async_computation.21 | async-start | bytes 8388608
  410.8 9.2 %slice-start.18 = ((s8[8388608]{0:T(1024)(128)(4,1)}), s8[4194304]{0:T(1024)(128)(4,1)S(1)}, s32[]{:S(2)}) async-start(s8[8388608]{0:T(1024)(128)(4,1)} %bitcast.190), calls=%async_computation.19 | async-start | bytes 8388608
  415.4 9.2 %slice-start.16 = ((s8[8388608]{0:T(1024)(128)(4,1)}), s8[4194304]{0:T(1024)(128)(4,1)S(1)}, s32[]{:S(2)}) async-start(s8[8388608]{0:T(1024)(128)(4,1)} %bitcast.187), calls=%async_computation.17 | async-start | bytes 8388608
  420.0 9.2 %slice-start.14 = ((s8[8388608]{0:T(1024)(128)(4,1)}), s8[4194304]{0:T(1024)(128)(4,1)S(1)}, s32[]{:S(2)}) async-start(s8[8388608]{0:T(1024)(128)(4,1)} %bitcast.184), calls=%async_computation.15 | async-start | bytes 8388608
  424.6 9.2 %slice-start.10 = ((s8[8388608]{0:T(1024)(128)(4,1)}), s8[4194304]{0:T(1024)(128)(4,1)S(1)}, s32[]{:S(2)}) async-start(s8[8388608]{0:T(1024)(128)(4,1)} %bitcast.178), calls=%async_computation.11 | async-start | bytes 8388608
  429.2 9.2 %slice-start.8 = ((s8[8388608]{0:T(1024)(128)(4,1)}), s8[4194304]{0:T(1024)(128)(4,1)S(1)}, s32[]{:S(2)}) async-start(s8[8388608]{0:T(1024)(128)(4,1)} %bitcast.175), calls=%async_computation.9 | async-start | bytes 8388608
  433.8 9.2 %slice-start.6 = ((s8[8388608]{0:T(1024)(128)(4,1)}), s8[4194304]{0:T(1024)(128)(4,1)S(1)}, s32[]{:S(2)}) async-start(s8[8388608]{0:T(1024)(128)(4,1)} %bitcast.172), calls=%async_computation.7 | async-start | bytes 8388608
  438.4 9.3 %slice-start.4 = ((s8[8388608]{0:T(1024)(128)(4,1)}), s8[4194304]{0:T(1024)(128)(4,1)S(1)}, s32[]{:S(2)}) async-start(s8[8388608]{0:T(1024)(128)(4,1)} %bitcast.169), calls=%async_computation.5 | async-start | bytes 8388608
  443.0 9.4 %slice-start.2 = ((s8[8388608]{0:T(1024)(128)(4,1)}), s8[4194304]{0:T(1024)(128)(4,1)S(1)}, s32[]{:S(2)}) async-start(s8[8388608]{0:T(1024)(128)(4,1)} %bitcast.166), calls=%async_computation.3 | async-start | bytes 8388608
  447.7 9.2 %slice-start.12 = ((s8[8388608]{0:T(1024)(128)(4,1)}), s8[4194304]{0:T(1024)(128)(4,1)S(1)}, s32[]{:S(2)}) async-start(s8[8388608]{0:T(1024)(128)(4,1)} %bitcast.181), calls=%async_computation.13 | async-start | bytes 8388608
  452.3 9.2 %slice-start.36 = ((s8[8388608]{0:T(1024)(128)(4,1)}), s8[4194304]{0:T(1024)(128)(4,1)S(1)}, s32[]{:S(2)}) async-start(s8[8388608]{0:T(1024)(128)(4,1)} %bitcast.217), calls=%async_computation.37 | async-start | bytes 8388608
  461.6 28.8 %slice-start.44 = ((s8[8388608]{0:T(1024)(128)(4,1)}), s8[4194304]{0:T(1024)(128)(4,1)S(1)}, s32[]{:S(2)}) async-start(s8[8388608]{0:T(1024)(128)(4,1)} %bitcast.232), calls=%async_computation.45 | async-start | bytes 8388608
  466.2 24.2 %slice-start.45 = ((s8[8388608]{0:T(1024)(128)(4,1)}), s8[4194304]{0:T(1024)(128)(4,1)S(1)}, s32[]{:S(2)}) async-start(s8[8388608]{0:T(1024)(128)(4,1)} %bitcast.232), calls=%async_computation.46 | async-start | bytes 8388608
  466.2 24.2 %copy-start.7 = (f32[64]{0:T(128)S(1)}, f32[64]{0:T(128)}, u32[]{:S(2)}) copy-start(f32[64]{0:T(128)} %convert_element_type.8) | copy-start | bytes 772
  (26 other events, 118.1 us)
Sparse Core Ops, SparseCore 0:
  8.9 58.3 all-gather.1
where the time goes:
time: 527 us; the launch traced here: 522 us
  local copies, waits for them, and re-layouts  169 us (32%)
  matrix products  163 us (31%)
  waiting for transfers between devices  144 us (27%)
  other arithmetic  26.5 us (5%)
  between operations  14 us (3%)
    dot_general x27, matrix products, convolve(): jnp.einsum('zpi,oi->zpo', window, tap_weight, preferred_element_type=jnp....  163 us
    slice x2, local copies, waits for them, and re-layouts, convolve(): framed[tap_z:tap_z + planes, tap_y:tap_y + rows, tap_x:tap_x + cols]  158 us
    ppermute x1, waiting for transfers between devices, extended(): lax.ppermute(tail, axis, [(i, (i + 1) % count) for i in range(ends)])  83.6 us
    all_gather x1, waiting for transfers between devices, body(): slab_planes = lax.all_gather(volume, 'filt', axis=0, tiled=True)  60 us
    concatenate x2, other arithmetic, extended(): jnp.concatenate([lax.ppermute(tail, axis, [(i, (i + 1) % count) for i in...  25.9 us
  transfers between devices with their start and end apart: 3, of which 2 were waited for; matrix products, arithmetic and copies ran while one was open for 1% of the time, Pallas kernels for 0%

commit v1 on v0

v1 whole, which is shorter than its diff:
```python
import functools

import jax
import jax.numpy as jnp
from jax import lax
from jax.experimental import pallas as pl
from jax.experimental.pallas import tpu as pltpu
from jax.sharding import PartitionSpec as P

CHUNKS = 16
MESH = pl.DeviceIdType.MESH


def kernel(slabs, vol_ref, w_ref, b_ref, out_ref, x, matrix, send, recv, local):
    rows, cols, chans = vol_ref.shape[1:]
    outs = out_ref.shape[-1]
    step_rows = rows // CHUNKS
    m = step_rows * cols
    v = lax.axis_index("vol")
    s = lax.axis_index("slab")
    f = lax.axis_index("filt")
    odd = lax.rem(f, 2)
    mate = f + 1 - 2 * odd
    across = lax.rem(f + 2, 4)
    diag = 3 - f
    outer = (f == 0) | (f == 3)
    has_prev = s > 0
    has_next = s < slabs - 1
    is_odd = odd == 1
    halo_to = s + 2 * odd - 1
    halo_slot = 5 - 5 * odd
    mate_slot = 5 * odd
    sends_halo = (is_odd & has_next) | (~is_odd & has_prev)
    takes_halo = (is_odd & has_prev) | (~is_odd & has_next)
    mate_halo = sends_halo

    def span(k):
        lo = 0 if k == 0 else step_rows * k + 1
        hi = rows if k == CHUNKS - 1 else step_rows * (k + 1) + 1
        return lo, hi - lo

    def own(k):
        lo, n = span(k)
        return vol_ref.at[0, pl.ds(lo, n)]

    def slot(z, k):
        lo, n = span(k)
        return x.at[z, pl.ds(lo + 1, n)]

    def remote(src, z, k, kind, dev):
        return pltpu.make_async_remote_copy(
            src_ref=src,
            dst_ref=slot(z, k),
            send_sem=send.at[kind, k],
            recv_sem=recv.at[z, k],
            device_id=dev,
            device_id_type=MESH,
        )

    to_across = (v, s, across)
    to_mate = (v, s, mate)
    to_halo = (v, halo_to, f)

    def c_y(k):
        return remote(own(k), f + 1, k, 0, to_across)

    def c_core(k):
        return remote(own(k), f + 1, k, 1, to_mate)

    def c_fwd(k):
        return remote(slot(across + 1, k), across + 1, k, 2, to_mate)

    def c_halo_own(k):
        return remote(own(k), halo_slot, k, 3, to_halo)

    def c_halo_fwd(k):
        return remote(slot(across + 1, k), halo_slot, k, 3, to_halo)

    def c_halo_mate(k):
        return remote(slot(halo_slot_in, k), halo_slot_in, k, 4, to_mate)

    halo_slot_in = halo_slot

    def c_local(k):
        return pltpu.make_async_copy(own(k), slot(f + 1, k), local.at[k])

    def arrived(z, k):
        remote(slot(z, k), z, k, 0, to_mate).wait_recv()

    barrier = pltpu.get_barrier_semaphore()
    pl.semaphore_signal(barrier, inc=1, device_id=to_mate, device_id_type=MESH)
    pl.semaphore_signal(barrier, inc=1, device_id=to_across, device_id_type=MESH)

    @pl.when(has_prev)
    def _():
        pl.semaphore_signal(barrier, inc=1, device_id=(v, s - 1, f), device_id_type=MESH)

    @pl.when(has_next)
    def _():
        pl.semaphore_signal(barrier, inc=1, device_id=(v, s + 1, f), device_id_type=MESH)

    inner = has_prev & has_next

    @pl.when(inner)
    def _():
        pl.semaphore_wait(barrier, 4)

    @pl.when(~inner)
    def _():
        pl.semaphore_wait(barrier, 3)

    for k in range(CHUNKS):
        c_y(k).start()

        @pl.when(outer & sends_halo)
        def _():
            c_halo_own(k).start()

        c_core(k).start()
        c_local(k).start()

    zero_row = jnp.zeros((cols, chans), x.dtype)
    for z in range(6):
        x[z, 0] = zero_row
        x[z, rows + 1] = zero_row

    def clear(z):
        @pl.loop(1, rows + 1)
        def _(r):
            x[z, r] = zero_row

    @pl.when(~has_prev)
    def _():
        clear(0)

    @pl.when(~has_next)
    def _():
        clear(5)

    for t in range(9):
        left, middle, right = (w_ref[3 * t + i] for i in range(3))
        tap = jnp.concatenate([middle, left, right, jnp.zeros_like(left)], axis=0)
        matrix[chans * t : chans * (t + 1)] = tap.T

    bias = b_ref[...].astype(jnp.float32)
    place = lax.rem(lax.broadcasted_iota(jnp.int32, (m, 2 * outs), 0), cols)

    def compute(k):
        @pl.loop(0, 4)
        def _(z):
            windows = [
                x[z + dz, pl.ds(step_rows * k + dy, step_rows)].reshape(m, chans)
                for dz in range(3)
                for dy in range(3)
            ]
            total = jnp.dot(
                jnp.concatenate(windows, axis=1), matrix[...], preferred_element_type=jnp.float32
            )
            near = total[:, : 2 * outs]
            far = total[:, 2 * outs :]
            before = jnp.where(place == 0, 0.0, pltpu.roll(near, 1, 0))
            after = jnp.where(place == cols - 1, 0.0, pltpu.roll(far, m - 1, 0))
            full = near + after + pltpu.roll(before, outs, 1)
            shifted = full[:, :outs] + bias
            result = jnp.where(shifted > 0, shifted, 0.3 * shifted)
            out_ref[z, pl.ds(step_rows * k, step_rows)] = result.astype(out_ref.dtype).reshape(
                step_rows, cols, outs
            )

    for t in range(CHUNKS + 2):
        k = t
        if k < CHUNKS:
            arrived(across + 1, k)
            c_fwd(k).start()

            @pl.when(~outer & sends_halo)
            def _():
                c_halo_fwd(k).start()

        k = t - 1
        if 0 <= k < CHUNKS:

            @pl.when(takes_halo)
            def _():
                arrived(halo_slot_in, k)
                c_halo_mate(k).start()

        k = t - 2
        if 0 <= k < CHUNKS:
            c_local(k).wait()
            arrived(mate + 1, k)
            arrived(diag + 1, k)

            @pl.when(mate_halo)
            def _():
                arrived(mate_slot, k)

            compute(k)

    for k in range(CHUNKS):
        c_y(k).wait_send()
        c_core(k).wait_send()
        c_fwd(k).wait_send()

        @pl.when(sends_halo)
        def _():
            c_halo_fwd(k).wait_send()

        @pl.when(takes_halo)
        def _():
            c_halo_mate(k).wait_send()


def body(volume, weights, bias):
    planes, rows, cols, chans = volume.shape
    outs = weights.shape[0]
    slabs = lax.axis_size("slab")
    depth = planes * lax.axis_size("filt")
    taps = weights.transpose(1, 0, 2)
    return pl.pallas_call(
        functools.partial(kernel, slabs),
        out_shape=jax.ShapeDtypeStruct((depth, rows, cols, outs), jnp.bfloat16),
        in_specs=[
            pl.BlockSpec(memory_space=pl.ANY),
            pl.BlockSpec(memory_space=pltpu.VMEM),
            pl.BlockSpec(memory_space=pltpu.VMEM),
        ],
        out_specs=pl.BlockSpec(memory_space=pltpu.VMEM),
        scratch_shapes=[
            pltpu.VMEM((depth + 2, rows + 2, cols, chans), jnp.bfloat16),
            pltpu.VMEM((9 * chans, 4 * outs), jnp.bfloat16),
            pltpu.SemaphoreType.DMA((5, CHUNKS)),
            pltpu.SemaphoreType.DMA((6, CHUNKS)),
            pltpu.SemaphoreType.DMA((CHUNKS,)),
        ],
        compiler_params=pltpu.CompilerParams(
            collective_id=0, has_side_effects=True, vmem_limit_bytes=50 * 1024 * 1024
        ),
        cost_estimate=pl.CostEstimate(
            flops=2 * depth * rows * cols * outs * 27 * chans,
            bytes_accessed=16 * rows * cols * chans,
            transcendentals=0,
        ),
    )(volume, taps, bias.reshape(1, outs))


def solution(mesh):
    return jax.shard_map(
        body,
        mesh=mesh,
        in_specs=(P(("vol", "slab", "filt"), None, None, None), P("filt", None, None), P("filt")),
        out_specs=P(("vol", "slab"), None, None, "filt"),
        check_vma=False,
    )
```

time: 527 us -> 90.6 us (0.17)
  matrix products: 163 us -> 0 us
  local copies, waits for them, and re-layouts: 169 us -> 8.57 us
  waiting for transfers between devices: 144 us -> 0 us
  Pallas kernels: 0 us -> 81.8 us
  other arithmetic: 26.5 us -> 0 us
  between operations: 14 us -> 0.01 us
    dot_general x27 -> x0, matrix products: 163 us -> none  [convolve(): jnp.einsum('zpi,oi->zpo', window, tap_weight, preferred_element_type=jnp....]
    slice x3 -> x0, local copies, waits for them, and re-layouts: 161 us -> none  [the longest x2 158 us: convolve(): framed[tap_z:tap_z + planes, tap_y:tap_y + rows, tap_x:tap_x + cols]]
    ppermute x2 -> x0, waiting for transfers between devices: 83.6 us -> none  [the longest x1 83.6 us: extended(): lax.ppermute(tail, axis, [(i, (i + 1) % count) for i in range(ends)])]
    pallas_call x0 -> x1, Pallas kernels: none -> 81.8 us  [body(): pl.pallas_call(functools.partial(kernel, slabs), out_shape=jax.ShapeDtype...]
    all_gather x1 -> x0, waiting for transfers between devices: 60 us -> none  [body(): slab_planes = lax.all_gather(volume, 'filt', axis=0, tiled=True)]
    concatenate x2 -> x0, other arithmetic: 25.9 us -> none  [extended(): jnp.concatenate([lax.ppermute(tail, axis, [(i, (i + 1) % count) for i in...]
    unnamed x110 -> x7, local copies, waits for them, and re-layouts: 2.95 us -> 8.57 us
  transfers between devices with their start and end apart: 3 -> 0, of which waited for: 2 -> 0; matrix products, arithmetic and copies ran while one was open for 1% -> 0% of each run, Pallas kernels for 0% -> 0%
where the time goes in v1:
time: 90.6 us; the launch traced here: 90.4 us
  Pallas kernels  81.8 us (90%)
  local copies, waits for them, and re-layouts  8.57 us (9%)
    pallas_call x1, Pallas kernels, body(): pl.pallas_call(functools.partial(kernel, slabs), out_shape=jax.ShapeDtype...  81.8 us
    unnamed x7, local copies, waits for them, and re-layouts  8.57 us

profile of v1, /device:TPU:4, one launch (start us, length us, event | category | flops | bytes accessed | tf_op | source)
XLA Modules:
  0.0 90.4 jit_solution(13705083908146275850)
XLA Ops:
  0.0 0.0 copy-start
  0.0 1.6 %copy-done = bf16[1,64,64,256]{3,2,1,0:T(8,128)(2,1)S(1)} copy-done((bf16[1,64,64,256]{3,2,1,0:T(8,128)(2,1)S(1)}, bf16[1,64,64,256]{3,2,1,0:T(8,128)(2,1)}, u32[]{:S(2)}) %copy-start) | copy-done | bytes 2097176
  1.6 0.0 copy-start.1
  1.6 1.2 %copy-done.1 = bf16[64,27,256]{2,0,1:T(8,128)(2,1)S(1)} copy-done((bf16[64,27,256]{2,0,1:T(8,128)(2,1)S(1)}, bf16[64,27,256]{2,0,1:T(8,128)(2,1)}, u32[]{:S(2)}) %copy-start.1) | copy-done | bytes 884760
  2.8 0.0 copy-start.2
  2.8 0.7 copy-done.2
  3.4 81.8 %shard_map.37 = bf16[4,64,64,64]{3,2,1,0:T(8,128)(2,1)} custom-call(bf16[1,64,64,256]{3,2,1,0:T(8,128)(2,1)S(1)} %copy-done, bf16[27,64,256]{2,1,0:T(8,128)(2,1)S(1)} %bitcast.2, bf16[1,64]{1,0:T(2,128)(2,1)S(1)} %bitcast.3), custom_call_target="tpu_custom_call" | custom-call | flops 14495514624 | bytes 16777216 | tf_op jit(solution)/shard_map/pallas_call | solution.py:220
  85.3 5.2 %copy.5 = bf16[4,64,64,64]{3,2,1,0:T(8,128)(2,1)} copy(bf16[4,64,64,64]{3,2,1,0:T(8,128)(2,1)} %shard_map.37) | data formatting | bytes 4194304
Async XLA Ops:
  0.0 1.6 %copy-start = (bf16[1,64,64,256]{3,2,1,0:T(8,128)(2,1)S(1)}, bf16[1,64,64,256]{3,2,1,0:T(8,128)(2,1)}, u32[]{:S(2)}) copy-start(bf16[1,64,64,256]{3,2,1,0:T(8,128)(2,1)} %vol_ref.1) | copy-start | bytes 6291460
  1.6 1.2 %copy-start.1 = (bf16[64,27,256]{2,0,1:T(8,128)(2,1)S(1)}, bf16[64,27,256]{2,0,1:T(8,128)(2,1)}, u32[]{:S(2)}) copy-start(bf16[64,27,256]{2,0,1:T(8,128)(2,1)} %param.4) | copy-start | bytes 2654212
  2.8 0.7 copy-start.2

commit v2 on v1

--- a/solution.py
+++ b/solution.py
@@ -7,15 +7,16 @@
 from jax.experimental.pallas import tpu as pltpu
 from jax.sharding import PartitionSpec as P
 
-CHUNKS = 16
+ENDS = (10, 20, 30, 39, 47, 54, 59, 62, 64)
+CHUNKS = len(ENDS)
 MESH = pl.DeviceIdType.MESH
 
 
-def kernel(slabs, vol_ref, w_ref, b_ref, out_ref, x, matrix, send, recv, local):
+def kernel(slabs, vol_ref, w_hbm, b_hbm, out_ref, x, matrix, w_ref, b_ref, send, recv, local, params):
     rows, cols, chans = vol_ref.shape[1:]
     outs = out_ref.shape[-1]
-    step_rows = rows // CHUNKS
-    m = step_rows * cols
+    ends = [rows * e // ENDS[-1] for e in ENDS]
+    begins = [0] + ends[:-1]
     v = lax.axis_index("vol")
     s = lax.axis_index("slab")
     f = lax.axis_index("filt")
@@ -35,8 +36,8 @@
     mate_halo = sends_halo
 
     def span(k):
-        lo = 0 if k == 0 else step_rows * k + 1
-        hi = rows if k == CHUNKS - 1 else step_rows * (k + 1) + 1
+        lo = 0 if k == 0 else begins[k] + 1
+        hi = rows if k == CHUNKS - 1 else ends[k] + 1
         return lo, hi - lo
 
     def own(k):
@@ -87,6 +88,11 @@
     def arrived(z, k):
         remote(slot(z, k), z, k, 0, to_mate).wait_recv()
 
+    get_w = pltpu.make_async_copy(w_hbm, w_ref, params.at[0])
+    get_b = pltpu.make_async_copy(b_hbm, b_ref, params.at[1])
+    get_w.start()
+    get_b.start()
+
     barrier = pltpu.get_barrier_semaphore()
     pl.semaphore_signal(barrier, inc=1, device_id=to_mate, device_id_type=MESH)
     pl.semaphore_signal(barrier, inc=1, device_id=to_across, device_id_type=MESH)
@@ -137,19 +143,24 @@
     def _():
         clear(5)
 
+    get_w.wait()
+    get_b.wait()
     for t in range(9):
         left, middle, right = (w_ref[3 * t + i] for i in range(3))
         tap = jnp.concatenate([middle, left, right, jnp.zeros_like(left)], axis=0)
         matrix[chans * t : chans * (t + 1)] = tap.T
 
     bias = b_ref[...].astype(jnp.float32)
-    place = lax.rem(lax.broadcasted_iota(jnp.int32, (m, 2 * outs), 0), cols)
 
     def compute(k):
+        step_rows = ends[k] - begins[k]
+        m = step_rows * cols
+        place = lax.rem(lax.broadcasted_iota(jnp.int32, (m, 2 * outs), 0), cols)
+
         @pl.loop(0, 4)
         def _(z):
             windows = [
-                x[z + dz, pl.ds(step_rows * k + dy, step_rows)].reshape(m, chans)
+                x[z + dz, pl.ds(begins[k] + dy, step_rows)].reshape(m, chans)
                 for dz in range(3)
                 for dy in range(3)
             ]
@@ -163,7 +174,7 @@
             full = near + after + pltpu.roll(before, outs, 1)
             shifted = full[:, :outs] + bias
             result = jnp.where(shifted > 0, shifted, 0.3 * shifted)
-            out_ref[z, pl.ds(step_rows * k, step_rows)] = result.astype(out_ref.dtype).reshape(
+            out_ref[z, pl.ds(begins[k], step_rows)] = result.astype(out_ref.dtype).reshape(
                 step_rows, cols, outs
             )
 
@@ -219,19 +230,22 @@
     taps = weights.transpose(1, 0, 2)
     return pl.pallas_call(
         functools.partial(kernel, slabs),
-        out_shape=jax.ShapeDtypeStruct((depth, rows, cols, outs), jnp.bfloat16),
+        out_shape=pltpu.VMEM((depth, rows, cols, outs), jnp.bfloat16),
         in_specs=[
-            pl.BlockSpec(memory_space=pl.ANY),
-            pl.BlockSpec(memory_space=pltpu.VMEM),
-            pl.BlockSpec(memory_space=pltpu.VMEM),
+            pl.BlockSpec(memory_space=pltpu.HBM),
+            pl.BlockSpec(memory_space=pltpu.HBM),
+            pl.BlockSpec(memory_space=pltpu.HBM),
         ],
         out_specs=pl.BlockSpec(memory_space=pltpu.VMEM),
         scratch_shapes=[
             pltpu.VMEM((depth + 2, rows + 2, cols, chans), jnp.bfloat16),
             pltpu.VMEM((9 * chans, 4 * outs), jnp.bfloat16),
+            pltpu.VMEM(taps.shape, jnp.bfloat16),
+            pltpu.VMEM((1, outs), jnp.bfloat16),
             pltpu.SemaphoreType.DMA((5, CHUNKS)),
             pltpu.SemaphoreType.DMA((6, CHUNKS)),
             pltpu.SemaphoreType.DMA((CHUNKS,)),
+            pltpu.SemaphoreType.DMA((2,)),
         ],
         compiler_params=pltpu.CompilerParams(
             collective_id=0, has_side_effects=True, vmem_limit_bytes=50 * 1024 * 1024

time: 90.6 us -> 70.1 us (0.77); the launches traced: 90.4 us -> 69 us
  Pallas kernels: 81.8 us -> 67 us
  local copies, waits for them, and re-layouts: 8.57 us -> 2.02 us
    pallas_call x1, Pallas kernels: 81.8 us -> 67 us  [body(): pl.pallas_call(functools.partial(kernel, slabs), out_shape=pltpu.VMEM((de...]
    unnamed x7 -> x1, local copies, waits for them, and re-layouts: 8.57 us -> 2.02 us
where the time goes in v2:
time: 70.1 us; the launch traced here: 69 us
  Pallas kernels  67 us (96%)
  local copies, waits for them, and re-layouts  2.02 us (3%)
    pallas_call x1, Pallas kernels, body(): pl.pallas_call(functools.partial(kernel, slabs), out_shape=pltpu.VMEM((de...  67 us
    unnamed x1, local copies, waits for them, and re-layouts  2.02 us

profile of v2, /device:TPU:4, one launch (start us, length us, event | category | flops | bytes accessed | tf_op | source)
XLA Modules:
  0.0 69.0 jit_solution(6022669805022962887)
XLA Ops:
  0.0 67.0 %shard_map.37 = bf16[4,64,64,64]{3,2,1,0:T(8,128)(2,1)S(1)} custom-call(bf16[1,64,64,256]{3,2,1,0:T(8,128)(2,1)} %vol_ref.1, bf16[27,64,256]{2,1,0:T(8,128)(2,1)} %bitcast.2, bf16[1,64]{1,0:T(2,128)(2,1)} %bitcast.3), custom_call_target="tpu_custom_call" | custom-call | flops 14495514624 | bytes 16777216 | tf_op jit(solution)/shard_map/pallas_call | solution.py:231
  67.0 2.0 %copy.5 = bf16[4,64,64,64]{3,2,1,0:T(8,128)(2,1)} copy(bf16[4,64,64,64]{3,2,1,0:T(8,128)(2,1)S(1)} %shard_map.37) | data formatting | bytes 4194304
